TPU v7x, 128 devices: a whole 4x4x4 slice. The times are simulated.
128 devices in a mesh: row: 8 (over z, core), col: 16 (over y, x).
Axes of the slice: x: 4, y: 4, z: 4, core: 2. Of those that a mesh axis runs over, the one named last changes fastest.
Arguments:
- parent_cov: bfloat16 [32768, 32768], P(('row', 'col')), may hold values from -6 to 6
- anc_index: int32 [16384], replicated, may hold values from 0 to 32767, as said below
- fac_rows: bfloat16 [16384, 2048], P('col'), may hold values from -0.125 to 0.125
- inv_factor: bfloat16 [2048, 2048], P(None, 'row'), may hold values from -0.125 to 0.125
- own_inverse: float32 [2048, 2048], P('row', 'col'), may hold values from -6 to 6
Outputs:
- cov_sa: float32 [2048, 16384], P('row', 'col')
- cov_ss: float32 [2048, 2048], P('row', 'col')
Inputs may be any that keep to these rules, and one draw needn't show every extreme that they name: `anc_index`: all values are distinct. Split the list into aligned blocks of 2048 entries and the values into ranges of 256 (one device's rows of parent_cov): no block holds more than 32 values of one range, and every block holds exactly 32 values of some range.
All inputs are finite; a program needn't handle non-finite values.
Results may differ from a plain program's by a relative error of at most 0.0049.
Values may be sent and summed in bfloat16 or wider, within the bound.
No kernel may reach another device: no remote copies, remote signals or barrier semaphores. Data moves between devices by JAX's collectives and lax.ppermute only.
A program may use at most 192 MiB of HBM per device.

v0:
```python
import jax
import jax.numpy as jnp
from jax import lax
from jax.sharding import PartitionSpec as P


def from_root(value, axis, source):
    kept = jnp.where(lax.axis_index(axis) == source, value, 0).astype(value.dtype)
    return lax.psum(kept, axis)


def inverse_order(order_ids):
    length = order_ids.shape[-1]
    positions = jnp.broadcast_to(jnp.arange(length, dtype=jnp.int32), order_ids.shape)
    result = jnp.zeros(order_ids.shape, jnp.int32)
    if order_ids.ndim == 1:
        return result.at[order_ids].set(positions)
    lines = jnp.broadcast_to(
        jnp.arange(order_ids.shape[0], dtype=jnp.int32)[:, None], order_ids.shape
    )
    return result.at[lines, order_ids].set(positions)


def local(parent_cov, anc_index, fac_rows, inv_factor, own_inverse):
    row_count = lax.axis_size("row")
    col_count = lax.axis_size("col")
    owners = row_count * col_count
    parent_rows = parent_cov.shape[0]
    ancestors = anc_index.shape[0]
    block_len = ancestors // row_count
    tile_cols = ancestors // col_count
    slot_cap = 2 * block_len // owners
    row_index = lax.axis_index("row")
    col_index = lax.axis_index("col")
    device = row_index * col_count + col_index
    owner_ids = anc_index // parent_rows
    is_mine = (owner_ids == device).astype(jnp.int32).reshape(row_count, block_len)
    mine_order = jnp.argsort(1 - is_mine, axis=1, stable=True)
    own_rank = inverse_order(mine_order)
    slot_ids = jnp.arange(row_count, dtype=jnp.int32)[:, None] * slot_cap + own_rank
    slot_ids = jnp.where(is_mine == 1, slot_ids, row_count * slot_cap)
    local_rows = (anc_index - device * parent_rows).reshape(row_count, block_len)
    slot_rows = jnp.full((row_count * slot_cap,), parent_rows, jnp.int32)
    slot_rows = slot_rows.at[slot_ids.reshape(-1)].set(local_rows.reshape(-1), mode="drop")
    picked_rows = jnp.take(parent_cov, slot_rows, axis=0, mode="fill", fill_value=0)
    picked = jnp.take(picked_rows, anc_index, axis=1)
    outgoing = picked.reshape(row_count, slot_cap, col_count, tile_cols).transpose(0, 2, 1, 3)
    flat_out = outgoing.reshape(owners * slot_cap, tile_cols)
    received = lax.all_to_all(flat_out, ("row", "col"), split_axis=0, concat_axis=0, tiled=True)
    block_ids = lax.dynamic_slice_in_dim(anc_index, row_index * block_len, block_len)
    sources = block_ids // parent_rows
    one_hot = (sources[:, None] == jnp.arange(owners, dtype=jnp.int32)[None, :]).astype(jnp.int32)
    per_owner = jnp.sum(one_hot, axis=0)
    owner_starts = jnp.cumsum(per_owner) - per_owner
    start_of = jnp.sum(one_hot * owner_starts[None, :], axis=1)
    source_order = jnp.argsort(sources, stable=True)
    slot_rank = inverse_order(source_order) - start_of
    cov_tile = jnp.take(received, sources * slot_cap + slot_rank, axis=0)
    sep_cols = inv_factor.shape[1]
    row_ids = jnp.arange(inv_factor.shape[0], dtype=jnp.int32)[:, None]
    col_ids = row_index * sep_cols + jnp.arange(sep_cols, dtype=jnp.int32)[None, :]
    lower = jnp.where(row_ids >= col_ids, inv_factor, jnp.zeros((), inv_factor.dtype))
    u_tile = jnp.dot(fac_rows, lower, preferred_element_type=jnp.float32).astype(jnp.bfloat16)
    u_cols = lax.all_gather(u_tile, "row", axis=1, tiled=True)
    groups = col_count // row_count
    panels = []
    for group in range(groups):
        panels.append(from_root(u_cols, "col", row_index * groups + group))
    u_block = jnp.concatenate(panels, axis=0)
    u_part = u_block
    cov_sa = lax.psum_scatter(
        -lax.dot_general(
            u_part, cov_tile, (((0,), (0,)), ((), ())), preferred_element_type=jnp.float32
        ),
        "row",
        scatter_dimension=0,
        tiled=True,
    )
    sa_rounded = cov_sa.astype(jnp.bfloat16)
    u_part = u_cols
    ss_block = lax.psum_scatter(
        lax.dot_general(
            u_part, sa_rounded, (((0,), (1,)), ((), ())), preferred_element_type=jnp.float32
        ),
        "col",
        scatter_dimension=0,
        tiled=True,
    )
    cov_ss = own_inverse - ss_block.T
    return (cov_sa, cov_ss)


def solution(mesh):
    return jax.shard_map(
        local,
        mesh=mesh,
        in_specs=(P(("row", "col"), None), P(), P("col", None), P(None, "row"), P("row", "col")),
        out_specs=(P("row", "col"), P("row", "col")),
        check_vma=False,
    )
```

profile of v0, /device:TPU:0, one launch (start us, length us, event | category | flops | bytes accessed | tf_op | source)
XLA Modules:
  0.0 706.0 jit_solution(9543739330395907756)
XLA Ops:
  8.1 0.9 fusion.22
  9.0 0.6 sub.42
  9.6 0.6 iota.45
  10.4 4.6 fusion.12
  15.3 0.5 sort.37.cloned.1.call-done
  15.7 0.8 fusion.20
  16.8 60.3 %scatter_custom_fusion.2 = s32[16384]{0:T(1024)S(1)} fusion(s32[16384]{0:T(1024)S(1)} %bitcast.40, s32[16384]{0:T(1024)S(1)} %bitcast.38, s32[]{:T(128)} %constant.94.clone.1), kind=kCustom, calls=%fused_computation.54 | custom fusion | bytes 65540
  77.4 60.5 %scatter_custom_fusion.1 = s32[256]{0:T(256)S(1)} fusion(s32[16384]{0:T(1024)S(1)} %bitcast.39, s32[16384]{0:T(1024)S(1)} %get-tuple-element.19, s32[]{:T(128)} %constant.90.clone.1), kind=kCustom, calls=%fused_computation.74 | custom fusion | bytes 1028 | tf_op jit(solution)/shard_map/scatter | solution.py:44
  138.0 39.0 %gather_fusion = bf16[256,32768]{1,0:T(8,128)(2,1)} fusion(bf16[256,32768]{1,0:T(8,128)(2,1)} %param.5, s32[1024]{0:T(1024)S(1)} %pad_clamp_fusion), kind=kCustom, calls=%fused_computation | custom fusion | bytes 33555456 | tf_op jit(solution)/shard_map/jit(_take)/gather | solution.py:45
  177.0 14.0 %broadcast_select_fusion = bf16[256,32768]{1,0:T(8,128)(2,1)} fusion(bf16[256,32768]{1,0:T(8,128)(2,1)} %gather_fusion, pred[256]{0:T(512)(128)(4,1)S(1)} %compare_and_fusion.2), kind=kLoop, calls=%fused_computation.6 | loop fusion | flops 8388608 | bytes 33554688 | tf_op jit(solution)/shard_map/jit(_take)/select_n | solution.py:45
  190.9 22.4 %copy.18 = bf16[256,32768]{0,1:T(8,128)(2,1)} copy(bf16[256,32768]{1,0:T(8,128)(2,1)} %broadcast_select_fusion) | data formatting | bytes 33554432 | tf_op jit(solution)/shard_map/jit(_take)/select_n | solution.py:45
  213.3 68.7 %gather_fusion.1 = bf16[16384,256]{1,0:T(8,128)(2,1)} fusion(bf16[256,32768]{0,1:T(8,128)(2,1)} %copy.18, s32[16384]{0:T(1024)S(1)} %get-tuple-element.18), kind=kCustom, calls=%fused_computation.1 | custom fusion | bytes 16842752 | tf_op jit(solution)/shard_map/jit(_take)/gather | solution.py:46
  282.1 12.3 %copy.19 = bf16[256,16384]{1,0:T(8,128)(2,1)} copy(bf16[256,16384]{0,1:T(8,128)(2,1)} %bitcast.36) | data formatting | bytes 16777216 | tf_op jit(solution)/shard_map/jit(_take)/gather | solution.py:46
  294.4 15.2 %copy.26 = bf16[32,8,16,1024]{3,2,1,0:T(8,128)(2,1)} copy(bf16[32,8,16,1024]{3,1,2,0:T(8,128)(2,1)} %bitcast.35) | data formatting | bytes 16777216
  309.6 6.0 broadcast_select_fusion.2
  315.6 7.4 %fusion = bf16[8,16,32,1024]{3,1,2,0:T(8,128)(2,1)} fusion(pred[16,1024]{1,0:T(8,128)(4,1)S(1)} %broadcast_in_dim.79, bf16[8,32,16,1024]{3,2,1,0:T(8,128)(2,1)} %bitcast.33), kind=kLoop, calls=%fused_computation.8 | loop fusion | flops 4194304 | bytes 16793600 | tf_op jit(solution)/shard_map/transpose | solution.py:47
  323.0 12.1 %copy.20 = bf16[8,16,32,1024]{3,2,1,0:T(8,128)(2,1)} copy(bf16[8,16,32,1024]{3,1,2,0:T(8,128)(2,1)} %fusion) | data formatting | bytes 16777216 | tf_op jit(solution)/shard_map/transpose | solution.py:47
  335.1 14.3 %all-to-all-start = ((bf16[128,32,1024]{2,1,0:T(8,128)(2,1)}), bf16[128,32,1024]{2,1,0:T(8,128)(2,1)}, u32[]{:S(2)}, u32[]{:S(2)}) async-start(bf16[128,32,1024]{2,1,0:T(8,128)(2,1)} %bitcast.34), calls=%async_computation | async-start | bytes 16777216 | tf_op jit(solution)/shard_map/all_to_all | solution.py:49
  349.5 0.4 convert_reduce_fusion
  350.0 0.2 reduce-window.8
  350.3 5.0 sort.34
  355.3 8.0 %scatter_custom_fusion = s32[2048]{0:T(1024)S(1)} fusion(s32[2048]{0:T(1024)S(1)} %compare_select_fusion.3, s32[2048]{0:T(1024)S(1)} %iota.43, s32[]{:T(128)} %constant.94.clone.1), kind=kCustom, calls=%fused_computation.68 | custom fusion | bytes 8196 | tf_op jit(solution)/shard_map/scatter | solution.py:17
  363.4 0.6 select_reduce_fusion
  364.1 107.5 %all-to-all-done = bf16[128,32,1024]{2,1,0:T(8,128)(2,1)} async-done(((bf16[128,32,1024]{2,1,0:T(8,128)(2,1)}), bf16[128,32,1024]{2,1,0:T(8,128)(2,1)}, u32[]{:S(2)}, u32[]{:S(2)}) %all-to-all-start) | async-done | bytes 8388640 | tf_op jit(solution)/shard_map/all_to_all | solution.py:49
  471.6 15.5 %gather_fusion.2 = bf16[2048,1024]{1,0:T(8,128)(2,1)} fusion(bf16[4096,1024]{1,0:T(8,128)(2,1)} %bitcast.7, s32[2048]{0:T(1024)S(1)} %broadcast_clamp_fusion), kind=kCustom, calls=%fused_computation.2 | custom fusion | bytes 8396800 | tf_op jit(solution)/shard_map/jit(_take)/gather | solution.py:58
  487.0 64.2 %all-reduce.3.cloned.1.call-done = (bf16[1024,2048]{0,1:T(8,128)(2,1)}, bf16[1024,2048]{0,1:T(8,128)(2,1)}) async-done(((bf16[1024,2048]{0,1:T(8,128)(2,1)}, bf16[1024,2048]{0,1:T(8,128)(2,1)}), (bf16[1024,2048]{0,1:T(8,128)(2,1)}, bf16[1024,2048]{0,1:T(8,128)(2,1)})) %all-reduce.3.cloned.1.call-update) | async-done | bytes 8388624 | tf_op jit(solution)/shard_map/psum | solution.py:9
  551.2 14.6 %fusion.5 = f32[2048,1024]{1,0:T(8,128)} fusion(bf16[1024,2048]{0,1:T(8,128)(2,1)} %get-tuple-element.12, bf16[1024,2048]{0,1:T(8,128)(2,1)} %get-tuple-element.13, bf16[2048,1024]{1,0:T(8,128)(2,1)} %gather_fusion.2, pred[2048]{0:T(1024)(128)(4,1)S(1)} %compare_and_fusion.1), kind=kOutput, calls=%fused_computation.13 | convolution fusion | flops 8610906112 | bytes 20973568 | tf_op jit(solution)/shard_map/dot_general | solution.py:72
  565.9 51.6 %reduce-scatter.3.cloned.1.call-done = f32[256,1024]{1,0:T(8,128)} async-done(((f32[2048,1024]{1,0:T(8,128)}), f32[256,1024]{1,0:T(8,128)}) %reduce-scatter.3.cloned.1.call-update) | async-done | bytes 1048592 | tf_op jit(solution)/shard_map/reduce_scatter | solution.py:71
  617.5 5.1 fusion.15
  622.7 73.7 %reduce-scatter.5.cloned.1.call-done = f32[128,256]{1,0:T(8,128)} async-done(((f32[2048,256]{1,0:T(8,128)}), f32[128,256]{1,0:T(8,128)}) %reduce-scatter.5.cloned.1.call-update) | async-done | bytes 131088 | tf_op jit(solution)/shard_map/reduce_scatter | solution.py:81
  696.5 0.9 bitcast_subtract_fusion
  697.4 0.8 copy.22
  (49 shorter events, 1.3 us)
Async XLA Ops:
  8.0 7.7 %sort.37.cloned.1.call-start = ((), (), s32[]{:S(2)}) async-start(), calls=%async_computation.7 | async-start | bytes 393248 | tf_op jit(solution)/shard_map/jit(argsort)/sort | solution.py:38
  10.3 299.4 %all-gather.2.cloned.1.call-start = ((), (), s32[]{:S(2)}) async-start(), calls=%async_computation.3 | async-start | bytes 4718592 | tf_op jit(solution)/shard_map/all_gather | solution.py:64
  10.3 4.8 copy-start
  10.3 6.3 copy-start.3
  10.4 6.3 copy-start.2
  15.0 536.2 %all-reduce.3.cloned.1.call-start = ((), (), s32[]{:S(2)}) async-start(), calls=%async_computation.6 | async-start | bytes 16777216 | tf_op jit(solution)/shard_map/psum | solution.py:9
  335.1 136.5 %all-to-all-start = ((bf16[128,32,1024]{2,1,0:T(8,128)(2,1)}), bf16[128,32,1024]{2,1,0:T(8,128)(2,1)}, u32[]{:S(2)}, u32[]{:S(2)}) async-start(bf16[128,32,1024]{2,1,0:T(8,128)(2,1)} %bitcast.34), calls=%async_computation | async-start | bytes 16777216 | tf_op jit(solution)/shard_map/all_to_all | solution.py:49
  349.4 268.0 %reduce-scatter.3.cloned.1.call-start = ((), (), s32[]{:S(2)}) async-start(), calls=%async_computation.4 | async-start | bytes 9437184 | tf_op jit(solution)/shard_map/reduce_scatter | solution.py:71
  565.8 56.8 %copy-start.1 = (f32[256,128]{1,0:T(8,128)S(1)}, f32[256,128]{1,0:T(8,128)}, u32[]{:S(2)}) copy-start(f32[256,128]{1,0:T(8,128)} %param.9) | copy-start | bytes 393220
  565.8 130.6 %reduce-scatter.5.cloned.1.call-start = ((), (), s32[]{:S(2)}) async-start(), calls=%async_computation.5 | async-start | bytes 2228224 | tf_op jit(solution)/shard_map/reduce_scatter | solution.py:81
Sparse Core Ops, SparseCore 0:
  12.0 3.4 sort.39.cloned.1.call-done
  (1 shorter events, 0.0 us)
Sparse Core Ops, SparseCore 1:
  15.1 34.6 all-gather.1
  315.7 235.5 all-reduce.2
  565.9 51.5 reduce-scatter.2
  622.7 73.7 reduce-scatter.4
where the time goes:
time: 712 us; the launch traced here: 706 us
  local copies, waits for them, and re-layouts  317 us (45%)
  waiting for transfers between devices  297 us (42%)
  other arithmetic  36.8 us (5%)
  matrix products  24.4 us (3%)
  between operations  16.2 us (2%)
  starting transfers between devices  14.5 us (2%)
    all_to_all x1, waiting for transfers between devices, local(): lax.all_to_all(flat_out, ('row', 'col'), split_axis=0, concat_axis=0, til...  107 us
    gather x2, local copies, waits for them, and re-layouts, local(): picked = jnp.take(picked_rows, anc_index, axis=1)  81.1 us
    unnamed x17, local copies, waits for them, and re-layouts  76.5 us
    reduce_scatter x1, waiting for transfers between devices, local(): lax.psum_scatter(lax.dot_general(u_part, sa_rounded, (((0,), (1,)), ((),...  73.7 us
    psum x1, waiting for transfers between devices, from_root(): return lax.psum(kept, axis)  64.2 us
    scatter x1, local copies, waits for them, and re-layouts, local(): slot_rows.at[slot_ids.reshape(-1)].set(local_rows.reshape(-1), mode='drop')  60.5 us
    reduce_scatter x1, waiting for transfers between devices, local(): lax.psum_scatter(-lax.dot_general(u_part, cov_tile, (((0,), (0,)), ((), (...  51.6 us
    gather x1, local copies, waits for them, and re-layouts, local(): jnp.take(parent_cov, slot_rows, axis=0, mode='fill', fill_value=0)  39 us
  transfers between devices with their start and end apart: 5, of which 4 were waited for; matrix products, arithmetic and copies ran while one was open for 49% of the time, Pallas kernels for 0%

commit v1 on v0

v1 whole, which is shorter than its diff:
```python
import functools

import jax
import jax.numpy as jnp
from jax import lax
from jax.experimental import pallas as pl
from jax.experimental.pallas import tpu as pltpu
from jax.sharding import PartitionSpec as P

BF = jnp.bfloat16
F32 = jnp.float32
SLOT = 32
LANES = 128
REACH = 10
WIN = 256


def dot_nt(a, b):
    return lax.dot_general(a, b, (((1,), (1,)), ((), ())), preferred_element_type=F32)


def one_hot(targets, base):
    ids = lax.broadcasted_iota(jnp.int32, (WIN, targets.shape[-1]), 0) + base
    return jnp.where(ids == targets, 1.0, 0.0).astype(BF)


def window_rows(table, data, lead, first, base):
    lines = [table[lead + (pl.ds(first + i, 1), slice(None))] for i in range(REACH)]
    hot = jnp.concatenate([one_hot(line, base) for line in lines], axis=1)
    start = pl.multiple_of(first * LANES, LANES)
    rows = data[lead + (pl.ds(start, REACH * LANES), slice(None))]
    return jnp.dot(hot, rows, preferred_element_type=F32)


def select_kernel(ranges, first_ref, count_ref, slots_ref, own_ref, table_ref, cov_ref, out_ref, held):
    step = pl.program_id(0)
    cols = slots_ref.shape[-1]
    blocks = held.shape[0]
    per_step = cov_ref.shape[1] // cols
    fill_steps = ranges // per_step

    @pl.when(step == 0)
    def _():
        extra = held.shape[1] - ranges * SLOT
        held[:, pl.ds(ranges * SLOT, extra), :] = jnp.zeros((blocks, extra, held.shape[2]), BF)

    @pl.when(step < fill_steps)
    def _():
        for k in range(per_step):
            hot = one_hot(slots_ref[k], 0)
            part = dot_nt(hot, cov_ref[:, k * cols:(k + 1) * cols]).astype(BF)
            at = pl.multiple_of((step * per_step + k) * SLOT, SLOT)
            for b in range(blocks):
                held[b, pl.ds(at, SLOT), :] = part[b * SLOT:(b + 1) * SLOT]

    @pl.when(step >= fill_steps)
    def _():
        tile = step - fill_steps
        block = tile // 2
        half = tile % 2
        windows = out_ref.shape[-1] // WIN
        rows_hot = one_hot(own_ref[0], 0)
        for w in range(windows):
            base = (half * windows + w) * WIN
            first = first_ref[tile, w]
            acc = window_rows(table_ref, held, (block,), first, base)

            def more(i, acc):
                return acc + window_rows(table_ref, held, (block,), first + i * REACH, base)

            acc = lax.fori_loop(1, count_ref[tile, w], more, acc)
            out = dot_nt(rows_hot, acc.astype(BF)).astype(BF)
            for b in range(blocks):
                out_ref[b, 0, :, w * WIN:(w + 1) * WIN] = out[b * SLOT:(b + 1) * SLOT]


def select(cov, slots, own, table, firsts, counts, tile_cols):
    rows, width = cov.shape
    ranges, _, cols = slots.shape
    blocks = table.shape[0]
    tiles = firsts.shape[0]
    per_step = 8
    fill = ranges // per_step
    grid_spec = pltpu.PrefetchScalarGridSpec(
        num_scalar_prefetch=2,
        grid=(fill + tiles,),
        in_specs=[
            pl.BlockSpec((per_step, 1, cols), lambda i, f, n: (jnp.minimum(i, fill - 1), 0, 0)),
            pl.BlockSpec((1, 1, cols), lambda i, f, n: (0, 0, 0)),
            pl.BlockSpec(table.shape, lambda i, f, n: (0, 0, 0)),
            pl.BlockSpec((rows, per_step * cols), lambda i, f, n: (0, jnp.minimum(i, fill - 1))),
        ],
        out_specs=pl.BlockSpec(
            (blocks, 1, SLOT, tile_cols), lambda i, f, n: (0, jnp.maximum(i - fill, 0), 0, 0)
        ),
        scratch_shapes=[pltpu.VMEM((blocks, ranges * SLOT + REACH * LANES, rows), BF)],
    )
    return pl.pallas_call(
        functools.partial(select_kernel, ranges),
        grid_spec=grid_spec,
        out_shape=jax.ShapeDtypeStruct((blocks, tiles, SLOT, tile_cols), BF),
        name="select_columns",
    )(firsts, counts, slots, own, table, cov)


def squeeze_kernel(first_ref, count_ref, table_ref, got_ref, out_ref, held, sem):
    rows = got_ref.shape[0]
    copy = pltpu.make_async_copy(got_ref, held.at[pl.ds(0, rows)], sem)
    copy.start()
    extra = held.shape[0] - rows
    held[pl.ds(rows, extra), :] = jnp.zeros((extra, held.shape[1]), BF)
    copy.wait()
    for w in range(out_ref.shape[0] // WIN):
        first = first_ref[w]
        acc = window_rows(table_ref, held, (), first, w * WIN)

        def more(i, acc, first=first, w=w):
            return acc + window_rows(table_ref, held, (), first + i * REACH, w * WIN)

        acc = lax.fori_loop(1, count_ref[w], more, acc)
        out_ref[w * WIN:(w + 1) * WIN, :] = acc.astype(BF)


def squeeze(received, table, firsts, counts, block_len):
    rows, cols = received.shape
    return pl.pallas_call(
        squeeze_kernel,
        in_specs=[
            pl.BlockSpec(memory_space=pltpu.SMEM),
            pl.BlockSpec(memory_space=pltpu.SMEM),
            pl.BlockSpec(memory_space=pltpu.VMEM),
            pl.BlockSpec(memory_space=pl.ANY),
        ],
        out_specs=pl.BlockSpec(memory_space=pltpu.VMEM),
        out_shape=jax.ShapeDtypeStruct((block_len, cols), BF),
        scratch_shapes=[pltpu.VMEM((rows + REACH * LANES, cols), BF), pltpu.SemaphoreType.DMA],
        name="squeeze_rows",
    )(firsts, counts, table, received)


def local(parent_cov, anc_index, fac_rows, inv_factor, own_inverse):
    row_count = lax.axis_size("row")
    col_count = lax.axis_size("col")
    owners = row_count * col_count
    parent_rows = parent_cov.shape[0]
    ancestors = anc_index.shape[0]
    block_len = ancestors // row_count
    tile_cols = ancestors // col_count
    row_index = lax.axis_index("row")
    col_index = lax.axis_index("col")
    device = row_index * col_count + col_index
    i32 = jnp.int32

    own_ids = lax.dynamic_slice_in_dim(anc_index, col_index * tile_cols, tile_cols)
    rank = jnp.sum((own_ids[None, :] < own_ids[:, None]).astype(i32), axis=1)
    perm = (jnp.arange(tile_cols, dtype=i32)[:, None] == rank[None, :]).astype(BF)
    sep_cols = inv_factor.shape[1]
    row_ids = jnp.arange(inv_factor.shape[0], dtype=i32)[:, None]
    col_ids = row_index * sep_cols + jnp.arange(sep_cols, dtype=i32)[None, :]
    lower = jnp.where(row_ids >= col_ids, inv_factor, jnp.zeros((), inv_factor.dtype))
    u_tile = jnp.dot(fac_rows, lower, preferred_element_type=F32).astype(BF)
    u_sorted = jnp.dot(perm, u_tile, preferred_element_type=F32).astype(BF)
    u_cols = lax.all_gather(u_sorted, "row", axis=1, tiled=True)
    share = tile_cols // row_count
    piece = lax.dynamic_slice_in_dim(u_cols, row_index * share, share, axis=0)
    moves = []
    for r in range(row_count):
        for c in range(col_count):
            target = (c // 2) * col_count + (c % 2) * row_count + r
            moves.append((r * col_count + c, target))
    piece = lax.ppermute(piece, ("row", "col"), moves)
    u_block = lax.all_gather(piece, "col", axis=0, tiled=True)

    owner_ids = anc_index // parent_rows
    inner_ids = anc_index % parent_rows
    tile_ids = (jnp.arange(ancestors, dtype=i32) // tile_cols + 1).astype(F32)
    owner_hot = jnp.where(
        owner_ids[None, :] == jnp.arange(owners, dtype=i32)[:, None], tile_ids[None, :], 0.0
    ).astype(BF)
    inner_hot = (inner_ids[:, None] == jnp.arange(parent_rows, dtype=i32)[None, :]).astype(BF)
    tile_of = jnp.dot(owner_hot, inner_hot, preferred_element_type=F32)
    masks = tile_of[None] == jnp.arange(1, col_count + 1, dtype=i32).astype(F32)[:, None, None]
    before = (
        jnp.arange(parent_rows, dtype=i32)[:, None] < jnp.arange(parent_rows, dtype=i32)[None, :]
    ).astype(BF)
    ahead = jnp.dot(
        masks.astype(BF).reshape(col_count * owners, parent_rows), before, preferred_element_type=F32
    ).reshape(col_count, owners, parent_rows)
    number = jnp.sum(masks.astype(F32), axis=2)
    tile_range = jnp.arange(col_count, dtype=i32)
    shifted = jnp.concatenate([jnp.zeros((1, owners), F32), number[:-1]], axis=0)
    base = (tile_range // 2 * SLOT).astype(F32)[:, None] + jnp.where(
        tile_range[:, None] % 2 == 1, shifted, 0.0
    )
    slots = jnp.sum(jnp.where(masks, ahead + base[:, :, None] + 1.0, 0.0), axis=0) - 1.0
    slots = slots.astype(i32).reshape(owners, 1, parent_rows)
    own_slots = lax.dynamic_slice_in_dim(slots, device, 1, axis=0)

    earlier = (
        jnp.arange(owners, dtype=i32)[:, None] < jnp.arange(owners, dtype=i32)[None, :]
    ).astype(BF)
    starts = jnp.dot(number.astype(BF), earlier, preferred_element_type=F32).astype(i32)
    number = number.astype(i32)
    s = jnp.arange(SLOT, dtype=i32)[None, None, :]
    n0, n1 = number[0::2, :, None], number[1::2, :, None]
    p0, p1 = starts[0::2, :, None], starts[1::2, :, None]
    table = jnp.where(s < n0, p0 + s, jnp.where(s < n0 + n1, tile_cols + p1 + s - n0, -1))
    table = table.reshape(row_count, owners * SLOT // LANES, LANES)
    table = jnp.pad(table, ((0, 0), (0, 16), (0, 0)), constant_values=-1)
    per_line = LANES // SLOT
    edges = jnp.arange(tile_cols // WIN, dtype=i32)[None, :, None] * WIN
    lead = jnp.sum((starts + number)[:, None, :] <= edges, axis=2, dtype=i32)
    last = jnp.sum(starts[:, None, :] < edges + WIN, axis=2, dtype=i32) - 1
    firsts = lead // per_line
    counts = (last // per_line - firsts) // REACH + 1

    outgoing = select(parent_cov, slots, own_slots, table, firsts, counts, tile_cols)
    flat_out = outgoing.reshape(owners * SLOT, tile_cols)
    received = lax.all_to_all(flat_out, ("row", "col"), split_axis=0, concat_axis=0, tiled=True)
    own_table = lax.dynamic_slice_in_dim(table, row_index, 1, axis=0)[0]
    own_firsts = lax.dynamic_slice_in_dim(firsts, row_index * 2, 2, axis=0).reshape(-1)
    own_counts = lax.dynamic_slice_in_dim(counts, row_index * 2, 2, axis=0).reshape(-1)
    cov_tile = squeeze(received, own_table, own_firsts, own_counts, block_len)

    part = lax.dot_general(
        u_block, cov_tile, (((0,), (0,)), ((), ())), preferred_element_type=F32
    )
    sa_sorted = lax.psum_scatter(
        (-part).astype(BF), "row", scatter_dimension=0, tiled=True
    ).astype(F32)
    sa_high = sa_sorted.astype(BF)
    ss_part = lax.dot_general(
        u_cols, sa_high, (((0,), (1,)), ((), ())), preferred_element_type=F32
    ).astype(BF)
    ss_all = lax.all_to_all(ss_part, "col", split_axis=0, concat_axis=0, tiled=True)
    sa_low = (sa_sorted - sa_high.astype(F32)).astype(BF)
    cov_sa = jnp.dot(sa_high, perm, preferred_element_type=F32) + jnp.dot(
        sa_low, perm, preferred_element_type=F32
    )
    ss_sum = jnp.sum(ss_all.reshape(col_count, -1, ss_all.shape[1]).astype(F32), axis=0)
    cov_ss = own_inverse - ss_sum.T
    return (cov_sa, cov_ss)


def solution(mesh):
    return jax.shard_map(
        local,
        mesh=mesh,
        in_specs=(P(("row", "col"), None), P(), P("col", None), P(None, "row"), P("row", "col")),
        out_specs=(P("row", "col"), P("row", "col")),
        check_vma=False,
    )
```

time: 712 us -> 367 us (0.52)
  local copies, waits for them, and re-layouts: 317 us -> 10.4 us
  waiting for transfers between devices: 297 us -> 188 us
  Pallas kernels: 0 us -> 61 us
  other arithmetic: 36.8 us -> 3.09 us
  starting transfers between devices: 14.5 us -> 46.9 us
  matrix products: 24.4 us -> 41.9 us
    gather x4 -> x0, local copies, waits for them, and re-layouts: 136 us -> none  [the longest x2 81.1 us: local(): picked = jnp.take(picked_rows, anc_index, axis=1)]
    reduce_scatter x2 -> x1, waiting for transfers between devices: 125 us -> 42.1 us  [local(): lax.psum_scatter((-part).astype(BF), 'row', scatter_dimension=0, tiled=True)]
    unnamed x17 -> x10, local copies, waits for them, and re-layouts: 76.5 us -> 1.65 us
    scatter x3 -> x0, local copies, waits for them, and re-layouts: 68.5 us -> none  [the longest x1 60.5 us: local(): slot_rows.at[slot_ids.reshape(-1)].set(local_rows.reshape(-1), mode='drop')]
    psum x1 -> x0, waiting for transfers between devices: 64.2 us -> none  [from_root(): return lax.psum(kept, axis)]
    pallas_call x0 -> x2, Pallas kernels: none -> 61 us  [the longest x1 46.5 us: select(): pl.pallas_call(functools.partial(select_kernel, ranges), grid_spec=grid_s...]
    all_gather x1 -> x2, waiting for transfers between devices: 0.01 us -> 38.9 us  [the longest x1 38.8 us: local(): u_cols = lax.all_gather(u_sorted, 'row', axis=1, tiled=True)]
    all_to_all x1, starting transfers between devices: 14.3 us -> 39.2 us  [local(): lax.all_to_all(flat_out, ('row', 'col'), split_axis=0, concat_axis=0, til...]
  transfers between devices with their start and end apart: 5 -> 6, of which waited for: 4 -> 4; matrix products, arithmetic and copies ran while one was open for 49% -> 7% of each run, Pallas kernels for 0% -> 17%
where the time goes in v1:
time: 367 us; the launch traced here: 365 us
  waiting for transfers between devices  188 us (51%)
  Pallas kernels  61 us (17%)
  starting transfers between devices  46.9 us (13%)
  matrix products  41.9 us (11%)
  between operations  14.1 us (4%)
  local copies, waits for them, and re-layouts  10.4 us (3%)
    all_to_all x1, waiting for transfers between devices, local(): lax.all_to_all(flat_out, ('row', 'col'), split_axis=0, concat_axis=0, til...  95.4 us
    pallas_call x1, Pallas kernels, select(): pl.pallas_call(functools.partial(select_kernel, ranges), grid_spec=grid_s...  46.5 us
    reduce_scatter x1, waiting for transfers between devices, local(): lax.psum_scatter((-part).astype(BF), 'row', scatter_dimension=0, tiled=True)  42.1 us
    all_to_all x1, starting transfers between devices, local(): lax.all_to_all(flat_out, ('row', 'col'), split_axis=0, concat_axis=0, til...  39.2 us
    all_gather x1, waiting for transfers between devices, local(): u_cols = lax.all_gather(u_sorted, 'row', axis=1, tiled=True)  38.8 us
    pallas_call x1, Pallas kernels, squeeze(): pl.pallas_call(squeeze_kernel, in_specs=[pl.BlockSpec(memory_space=pltpu....  14.5 us
    dot_general x1, matrix products, local(): lax.dot_general(u_block, cov_tile, (((0,), (0,)), ((), ())), preferred_el...  14 us
    dot_general x1, matrix products, local(): tile_of = jnp.dot(owner_hot, inner_hot, preferred_element_type=F32)  13.9 us
  transfers between devices with their start and end apart: 6, of which 4 were waited for; matrix products, arithmetic and copies ran while one was open for 7% of the time, Pallas kernels for 17%

profile of v1, /device:TPU:0, one launch (start us, length us, event | category | flops | bytes accessed | tf_op | source)
XLA Modules:
  0.0 365.2 jit_solution(7691583656952219624)
XLA Ops:
  7.2 0.7 dynamic_slice.18
  7.9 0.6 convert_reduce_fusion
  8.5 5.4 %fusion.19 = bf16[1024,256]{1,0:T(8,128)(2,1)} fusion(s32[1024]{0:T(1024)S(1)} %convert_reduce_fusion, bf16[1024,2048]{1,0:T(8,128)(2,1)} %param.7, bf16[2048,256]{1,0:T(8,128)(2,1)} %param.8, s32[256]{0:T(256)S(1)} %iota_add_fusion), kind=kOutput, calls=%fused_computation.28 | convolution fusion | flops 1613234176 | bytes 5772288 | tf_op jit(solution)/shard_map/dot_general | solution.py:162
  14.0 38.8 %all-gather.3.cloned.1.call-done = bf16[1024,2048]{1,0:T(8,128)(2,1)} async-done(((bf16[1024,256]{1,0:T(8,128)(2,1)}), bf16[1024,2048]{1,0:T(8,128)(2,1)}) %all-gather.3.cloned.1.call-update) | async-done | bytes 4194320 | tf_op jit(solution)/shard_map/all_gather | solution.py:163
  52.8 1.1 constant_dynamic-slice_fusion.3
  53.9 0.7 collective-permute-start
  54.6 0.8 copy-done
  55.6 0.8 select_convert_fusion.5
  56.4 13.9 %fusion = f32[128,256]{1,0:T(8,128)S(1)} fusion(s32[16384]{0:T(1024)S(1)} %get-tuple-element.7, bf16[128,16384]{1,0:T(8,128)(2,1)S(1)} %select_convert_fusion.5), kind=kOutput, calls=%fused_computation.1 | convolution fusion | flops 1077936128 | bytes 4390912 | tf_op jit(solution)/shard_map/dot_general | solution.py:181
  70.3 0.4 fusion.10
  73.0 0.8 fusion.11
  73.8 0.7 convert_element_type.101.slots_ref
  74.6 0.7 pad.5.table_ref
  75.3 0.6 fusion.45.own_ref
  75.9 0.6 fusion.40
  76.5 46.5 %select_columns.1 = bf16[8,16,32,1024]{3,2,1,0:T(8,128)(2,1)} custom-call(s32[16,4]{1,0:T(8,128)} %get-tuple-element.9.first_ref, s32[16,4]{1,0:T(8,128)} %get-tuple-element.8.count_ref, s32[128,1,256]{2,1,0:T(1,128)} %convert_element_type.101.slots_ref, s32[1,1,256]{2,1,0:T(1,128)} %fusion.45.own_ref, s32[8,48,128]{2,1,0:T(8,128)} %pad.5.table_ref, ...), custom_call_target="tpu_custom_call" | custom-call | tf_op jit(solution)/shard_map/select_columns/pallas_call | solution.py:98
  123.0 39.2 %all-to-all-start = ((bf16[128,32,1024]{2,1,0:T(8,128)(2,1)}), bf16[128,32,1024]{2,1,0:T(8,128)(2,1)}, u32[]{:S(2)}, u32[]{:S(2)}) async-start(bf16[128,32,1024]{2,1,0:T(8,128)(2,1)} %bitcast.20), calls=%async_computation | async-start | bytes 16777216 | tf_op jit(solution)/shard_map/all_to_all | solution.py:219
  162.3 0.7 constant_dynamic-slice_fusion.1
  163.0 0.7 reshape.138.count_ref
  163.6 0.7 constant_dynamic-slice_fusion.2
  164.3 0.7 reshape.137.first_ref
  165.0 0.6 dynamic-slice_bitcast_fusion.table_ref
  165.6 95.4 %all-to-all-done = bf16[128,32,1024]{2,1,0:T(8,128)(2,1)} async-done(((bf16[128,32,1024]{2,1,0:T(8,128)(2,1)}), bf16[128,32,1024]{2,1,0:T(8,128)(2,1)}, u32[]{:S(2)}, u32[]{:S(2)}) %all-to-all-start) | async-done | bytes 8388640 | tf_op jit(solution)/shard_map/all_to_all | solution.py:219
  261.0 14.5 %squeeze_rows.1 = bf16[2048,1024]{1,0:T(8,128)(2,1)} custom-call(s32[8]{0:T(128)} %reshape.137.first_ref, s32[8]{0:T(128)} %reshape.138.count_ref, s32[48,128]{1,0:T(8,128)} %dynamic-slice_bitcast_fusion.table_ref, bf16[4096,1024]{1,0:T(8,128)(2,1)} %bitcast.4.got_ref), custom_call_target="tpu_custom_call" | custom-call | tf_op jit(solution)/shard_map/squeeze_rows/pallas_call | solution.py:126
  275.5 14.0 %negate_convert_fusion = bf16[2048,1024]{1,0:T(8,128)(2,1)} fusion(bf16[2048,2048]{1,0:T(8,128)(2,1)} %all-gather.5.cloned.1.call-done, bf16[2048,1024]{1,0:T(8,128)(2,1)} %squeeze_rows.1), kind=kOutput, calls=%fused_computation.2 | convolution fusion | flops 8594128896 | bytes 16777216 | tf_op jit(solution)/shard_map/dot_general | solution.py:225
  289.6 42.1 %reduce-scatter.2.cloned.1.call-done = bf16[256,1024]{1,0:T(8,128)(2,1)} async-done(((bf16[2048,1024]{1,0:T(8,128)(2,1)}), bf16[256,1024]{1,0:T(8,128)(2,1)}) %reduce-scatter.2.cloned.1.call-update) | async-done | bytes 524304 | tf_op jit(solution)/shard_map/reduce_scatter | solution.py:228
  331.7 4.7 %convolution_convert_fusion = bf16[2048,256]{1,0:T(8,128)(2,1)} fusion(bf16[1024,2048]{1,0:T(8,128)(2,1)} %all-gather.3.cloned.1.call-done, bf16[256,1024]{1,0:T(8,128)(2,1)} %reduce-scatter.2.cloned.1.call-done), kind=kOutput, calls=%fused_computation.18 | convolution fusion | flops 1074266112 | bytes 5767168 | tf_op jit(solution)/shard_map/dot_general | solution.py:232
  336.4 6.9 %all-to-all-start.1 = ((bf16[16,128,256]{2,1,0:T(8,128)(2,1)}), bf16[16,128,256]{2,1,0:T(8,128)(2,1)S(1)}, u32[]{:S(2)}, u32[]{:S(2)}) async-start(bf16[16,128,256]{2,1,0:T(8,128)(2,1)} %bitcast.5), calls=%async_computation.2 | async-start | bytes 2097152 | tf_op jit(solution)/shard_map/all_to_all | solution.py:235
  343.4 1.0 fusion.5
  344.4 2.0 fusion.18
  346.4 11.4 %all-to-all-done.1 = bf16[16,128,256]{2,1,0:T(8,128)(2,1)S(1)} async-done(((bf16[16,128,256]{2,1,0:T(8,128)(2,1)}), bf16[16,128,256]{2,1,0:T(8,128)(2,1)S(1)}, u32[]{:S(2)}, u32[]{:S(2)}) %all-to-all-start.1) | async-done | bytes 1048608 | tf_op jit(solution)/shard_map/all_to_all | solution.py:235
  358.0 0.8 copy.15
  (50 shorter events, 2.9 us)
Async XLA Ops:
  7.2 45.7 %all-gather.3.cloned.1.call-start = ((), (), s32[]{:S(2)}) async-start(), calls=%async_computation.3 | async-start | bytes 4718592 | tf_op jit(solution)/shard_map/all_gather | solution.py:163
  8.5 47.0 %copy-start.2 = (s32[16384]{0:T(1024)S(1)}, s32[16384]{0:T(1024)}, u32[]{:S(2)}) copy-start(s32[16384]{0:T(1024)} %param.6) | copy-start | bytes 196612
  13.9 261.6 %all-gather.5.cloned.1.call-start = ((), (), s32[]{:S(2)}) async-start(), calls=%async_computation.4 | async-start | bytes 8912896 | tf_op jit(solution)/shard_map/all_gather | solution.py:172
  53.9 0.7 collective-permute-start
  54.6 0.8 copy-start
  123.0 138.0 %all-to-all-start = ((bf16[128,32,1024]{2,1,0:T(8,128)(2,1)}), bf16[128,32,1024]{2,1,0:T(8,128)(2,1)}, u32[]{:S(2)}, u32[]{:S(2)}) async-start(bf16[128,32,1024]{2,1,0:T(8,128)(2,1)} %bitcast.20), calls=%async_computation | async-start | bytes 16777216 | tf_op jit(solution)/shard_map/all_to_all | solution.py:219
  162.2 169.5 %reduce-scatter.2.cloned.1.call-start = ((), (), s32[]{:S(2)}) async-start(), calls=%async_computation.5 | async-start | bytes 4718592 | tf_op jit(solution)/shard_map/reduce_scatter | solution.py:228
  289.5 53.7 %copy-start.1 = (f32[256,128]{1,0:T(8,128)S(1)}, f32[256,128]{1,0:T(8,128)}, u32[]{:S(2)}) copy-start(f32[256,128]{1,0:T(8,128)} %param.9) | copy-start | bytes 393220
  331.7 11.7 %copy-start.3 = (bf16[256,1024]{1,0:T(8,128)(2,1)S(1)}, bf16[256,1024]{1,0:T(8,128)(2,1)}, u32[]{:S(2)}) copy-start(bf16[256,1024]{1,0:T(8,128)(2,1)} %reduce-scatter.2.cloned.1.call-done) | copy-start | bytes 1572868
  336.4 21.4 %all-to-all-start.1 = ((bf16[16,128,256]{2,1,0:T(8,128)(2,1)}), bf16[16,128,256]{2,1,0:T(8,128)(2,1)S(1)}, u32[]{:S(2)}, u32[]{:S(2)}) async-start(bf16[16,128,256]{2,1,0:T(8,128)(2,1)} %bitcast.5), calls=%async_computation.2 | async-start | bytes 2097152 | tf_op jit(solution)/shard_map/all_to_all | solution.py:235
Sparse Core Ops, SparseCore 0:
  14.1 38.7 all-gather.2
  55.6 100.3 all-gather.4
  289.7 41.9 reduce-scatter.1
